TPU v7x, 32 devices: a whole 2x2x4 slice. The times are simulated.
32 devices in a mesh: row: 8 (over z, y), col: 4 (over x, core).
Axes of the slice: x: 2, y: 2, z: 4, core: 2. Of those that a mesh axis runs over, the one named last changes fastest.
Arguments:
- rhs_grid: float32 [65536, 512], P(('row', 'col')), may hold values from -6 to 6
- leaf_order: int32 [128, 512], P(('row', 'col')), may hold values from 0 to 511, each once within a row
- source_basis: float32 [128, 512, 192], P(('row', 'col')), may hold values from -0.25 to 0.25
- transfer: float32 [7, 128, 192, 384], P(None, ('row', 'col')), may hold values from -0.3125 to 0.3125
- target_basis: float32 [128, 512, 192], P(('row', 'col')), may hold values from -0.4375 to 0.4375
Outputs:
- result: float32 [65536, 512], P(('row', 'col'))
Inputs may be any that keep to these rules, and one draw needn't show every extreme that they name: Each row of leaf_order names every one of 0 to 511 once.
All inputs are finite; a program needn't handle non-finite values.
Results may differ from a plain program's by a relative error of at most 0.00013.
Values sent between devices are 32-bit elements; how exact they have to be, the bound alone decides.
A program may use at most 128 MiB of HBM per device.

v0:
```python
import jax
import jax.numpy as jnp
from jax import lax
from jax.sharding import PartitionSpec as P

PRECISE = lax.Precision.HIGHEST


def from_partner(value, axis, apart):
    mask = 2**apart
    pairs = [(source, source ^ mask) for source in range(lax.axis_size(axis))]
    return lax.ppermute(value, axis, pairs)


def partner_of(values, bit_pos):
    node_count = values.shape[0]
    halves = values.reshape((node_count // 2 ** (bit_pos + 1), 2, 2**bit_pos) + values.shape[1:])
    return halves[:, ::-1].reshape(values.shape)


def combine(blocks, own, other):
    skel_size = own.shape[1]
    own_term = jnp.einsum("nij,njr->nir", blocks[:, :, :skel_size], own, precision=PRECISE)
    return own_term + jnp.einsum("nij,njr->nir", blocks[:, :, skel_size:], other, precision=PRECISE)


def place_rows(basis, order):

    def single(leaf_block, leaf_index):
        return jnp.zeros_like(leaf_block).at[leaf_index].set(leaf_block)

    return jax.vmap(single)(basis, order)


def on_device(rhs_grid, leaf_order, source_basis, transfer, target_basis):
    leaf_count, leaf_rows = leaf_order.shape
    columns = rhs_grid.shape[1]
    low_bits = leaf_count.bit_length() - 1
    row_bits = lax.axis_size("row").bit_length() - 1
    col_count = lax.axis_size("col")
    col_bits = col_count.bit_length() - 1
    first_col = low_bits + row_bits
    placed_in = place_rows(source_basis, leaf_order)
    skeleton = jnp.einsum(
        "lqk,lqr->lkr",
        placed_in,
        rhs_grid.reshape(leaf_count, leaf_rows, columns),
        precision=PRECISE,
    )
    current = skeleton
    for section in range(low_bits):
        current = combine(transfer[section], current, partner_of(current, section))
    for bit_pos in range(row_bits):
        remote = from_partner(current, "row", bit_pos)
        current = combine(transfer[low_bits + bit_pos], current, remote)
    for bit_pos in range(col_bits):
        remote = from_partner(current, "col", bit_pos)
        current = combine(transfer[first_col + bit_pos], current, remote)
    skeleton = current
    placed_out = place_rows(target_basis, leaf_order)
    result = jnp.einsum("lqk,lkr->lqr", placed_out, skeleton, precision=PRECISE)
    return result.reshape(leaf_count * leaf_rows, columns)


def solution(mesh):
    in_specs = (
        P(("row", "col"), None),
        P(("row", "col"), None),
        P(("row", "col"), None, None),
        P(None, ("row", "col"), None, None),
        P(("row", "col"), None, None),
    )
    out_specs = P(("row", "col"), None)
    return jax.shard_map(
        on_device, mesh=mesh, in_specs=in_specs, out_specs=out_specs, check_vma=False
    )
```

profile of v0, /device:TPU:0, one launch (start us, length us, event | category | flops | bytes accessed | tf_op | source)
XLA Modules:
  0.0 242.9 jit_solution(11124845153787148813)
XLA Ops:
  0.0 6.3 %slice_bitcast_fusion = (f32[4,192,384]{2,1,0:T(8,128)S(1)}, f32[4,192,384]{2,1,0:T(8,128)}, f32[4,192,384]{2,1,0:T(8,128)}, f32[4,192,384]{2,1,0:T(8,128)}, f32...) fusion(f32[7,4,192,384]{3,2,1,0:T(8,128)} %param.8), kind=kLoop, calls=%fused_computation.10 | loop fusion | bytes 16515072 | tf_op jit(solution)/shard_map/squeeze | solution.py:58
  6.6 1.8 copy.21
  8.4 10.4 %scatter_custom_fusion.1 = f32[2048,192]{1,0:T(8,128)} fusion(s32[2048]{0:T(1024)S(1)} %bitcast.66, f32[2048,192]{1,0:T(8,128)S(1)} %bitcast.65, f32[]{:T(128)} %constant.0.clone.1), kind=kCustom, calls=%fused_computation.17 | custom fusion | bytes 1572868
  18.9 9.7 %fusion.29 = f32[4,192,512]{2,1,0:T(8,128)S(1)} fusion(f32[4,512,192]{2,1,0:T(8,128)} %bitcast.56, f32[4,512,512]{2,1,0:T(8,128)} %bitcast.63), kind=kOutput, calls=%fused_computation.49 | convolution fusion | flops 2415919104 | bytes 7340032 | tf_op jit(solution)/shard_map/lqk,lqr->lkr/dot_general | solution.py:44
  28.6 2.7 %fusion.26 = f32[4,512,192]{1,2,0:T(8,128)} fusion(f32[4,192,512]{2,1,0:T(8,128)S(1)} %fusion.29, f32[4,192,384]{2,1,0:T(8,128)S(1)} %copy-done.5), kind=kOutput, calls=%fused_computation.41 | convolution fusion | flops 905969664 | bytes 3932160 | tf_op jit(solution)/shard_map/nij,njr->nir/dot_general | solution.py:23
  32.6 3.8 %convolution_add_fusion.5 = f32[4,512,192]{1,2,0:T(8,128)S(1)} fusion(f32[4,512,192]{1,2,0:T(8,128)} %fusion.26, f32[4,192,512]{2,1,0:T(8,128)} %bitcast.57, f32[4,192,384]{2,1,0:T(8,128)} %get-tuple-element.10), kind=kOutput, calls=%fused_computation.9 | convolution fusion | flops 906362880 | bytes 5505024 | tf_op jit(solution)/shard_map/nij,njr->nir/dot_general | solution.py:24
  36.4 2.7 %fusion.23 = f32[4,512,192]{1,2,0:T(8,128)} fusion(f32[4,512,192]{1,2,0:T(8,128)S(1)} %convolution_add_fusion.5, f32[4,192,384]{2,1,0:T(8,128)S(1)} %copy-done.4), kind=kOutput, calls=%fused_computation.38 | convolution fusion | flops 905969664 | bytes 3932160 | tf_op jit(solution)/shard_map/nij,njr->nir/dot_general | solution.py:23
  40.4 3.9 %convolution_add_fusion.4 = f32[4,512,192]{1,2,0:T(8,128)S(1)} fusion(f32[4,512,192]{1,2,0:T(8,128)} %fusion.23, f32[4,192,512]{2,1,0:T(8,128)} %bitcast.58, f32[4,192,384]{2,1,0:T(8,128)} %get-tuple-element.9), kind=kOutput, calls=%fused_computation.8 | convolution fusion | flops 906362880 | bytes 5505024 | tf_op jit(solution)/shard_map/nij,njr->nir/dot_general | solution.py:24
  44.3 3.1 %collective-permute-start = (f32[4,192,512]{2,1,0:T(8,128)S(1)}, f32[4,192,512]{2,1,0:T(8,128)S(1)}, u32[]{:S(2)}, u32[]{:S(2)}) collective-permute-start(f32[4,192,512]{2,1,0:T(8,128)S(1)} %bitcast.59), channel_id=1, source_target_pairs={{0,4},{4,0},{8,12},{12,8},{16,20},{20,16},{24,28},{28,24},{1,5},{5... | collective-permute-start | bytes 4718600 | tf_op jit(solution)/shard_map/ppermute | solution.py:12
  49.0 32.8 %collective-permute-done = f32[4,192,512]{2,1,0:T(8,128)S(1)} collective-permute-done((f32[4,192,512]{2,1,0:T(8,128)S(1)}, f32[4,192,512]{2,1,0:T(8,128)S(1)}, u32[]{:S(2)}, u32[]{:S(2)}) %collective-permute-start) | collective-permute-done | bytes 1572896 | tf_op jit(solution)/shard_map/ppermute | solution.py:12
  83.4 1.9 collective-permute-start.1
  86.8 32.1 %collective-permute-done.1 = f32[4,192,512]{2,1,0:T(8,128)S(1)} collective-permute-done((f32[4,192,512]{2,1,0:T(8,128)S(1)}, f32[4,192,512]{2,1,0:T(8,128)S(1)}, u32[]{:S(2)}, u32[]{:S(2)}) %collective-permute-start.1) | collective-permute-done | bytes 1572896 | tf_op jit(solution)/shard_map/ppermute | solution.py:12
  119.0 1.8 convolution_add_fusion.2
  120.8 2.6 %collective-permute-start.2 = (f32[4,192,512]{2,1,0:T(8,128)S(1)}, f32[4,192,512]{2,1,0:T(8,128)S(1)}, u32[]{:S(2)}, u32[]{:S(2)}) collective-permute-start(f32[4,192,512]{2,1,0:T(8,128)S(1)} %bitcast.61), channel_id=1, source_target_pairs={{0,16},{4,20},{8,24},{12,28},{16,0},{20,4},{24,8},{28,12},{1,17},{... | collective-permute-start | bytes 4718600 | tf_op jit(solution)/shard_map/ppermute | solution.py:12
  125.0 65.2 %collective-permute-done.2 = f32[4,192,512]{2,1,0:T(8,128)S(1)} collective-permute-done((f32[4,192,512]{2,1,0:T(8,128)S(1)}, f32[4,192,512]{2,1,0:T(8,128)S(1)}, u32[]{:S(2)}, u32[]{:S(2)}) %collective-permute-start.2) | collective-permute-done | bytes 1572896 | tf_op jit(solution)/shard_map/ppermute | solution.py:12
  190.2 1.6 convolution_add_fusion.1
  193.5 1.8 collective-permute-done.3
  195.3 2.8 %convolution_add_fusion = f32[4,512,192]{1,2,0:T(8,128)} fusion(f32[4,512,192]{1,2,0:T(8,128)S(1)} %fusion.11, f32[4,192,512]{2,1,0:T(8,128)S(1)} %collective-permute-done.3, f32[4,192,384]{2,1,0:T(8,128)S(1)} %copy-done), kind=kOutput, calls=%fused_computation.4 | convolution fusion | flops 906362880 | bytes 5505024 | tf_op jit(solution)/shard_map/nij,njr->nir/dot_general | solution.py:24
  199.3 1.8 copy.18
  201.0 10.2 %scatter_custom_fusion = f32[2048,192]{1,0:T(8,128)S(1)} fusion(s32[2048]{0:T(1024)S(1)} %bitcast.67, f32[2048,192]{1,0:T(8,128)} %bitcast.64, f32[]{:T(128)} %constant.0.clone.1), kind=kCustom, calls=%fused_computation.19 | custom fusion | bytes 1573376
  211.3 3.0 %fusion.8 = f32[4,512,192]{1,2,0:T(8,128)S(1)} fusion(f32[4,512,192]{1,2,0:T(8,128)} %convolution_add_fusion, f32[4,192,384]{2,1,0:T(8,128)S(1)} %get-tuple-element.5), kind=kOutput, calls=%fused_computation.23 | convolution fusion | flops 905969664 | bytes 3932160 | tf_op jit(solution)/shard_map/nij,njr->nir/dot_general | solution.py:23
  214.3 20.6 %collective-permute-done.4 = f32[4,192,512]{2,1,0:T(8,128)} collective-permute-done((f32[4,192,512]{2,1,0:T(8,128)}, f32[4,192,512]{2,1,0:T(8,128)}, u32[]{:S(2)}, u32[]{:S(2)}) %collective-permute-start.4) | collective-permute-done | bytes 1572896 | tf_op jit(solution)/shard_map/ppermute | solution.py:12
  234.9 3.0 %fusion.6 = f32[4,512,192]{1,2,0:T(8,128)S(1)} fusion(f32[4,192,512]{2,1,0:T(8,128)} %collective-permute-done.4, f32[4,192,384]{2,1,0:T(8,128)S(1)} %get-tuple-element.5), kind=kOutput, calls=%fused_computation.21 | convolution fusion | flops 905969664 | bytes 3932160 | tf_op jit(solution)/shard_map/nij,njr->nir/dot_general | solution.py:24
  237.9 5.0 %fusion = f32[4,512,512]{2,1,0:T(8,128)} fusion(f32[4,512,192]{2,1,0:T(8,128)S(1)} %bitcast.55, f32[4,512,192]{1,2,0:T(8,128)S(1)} %fusion.8, f32[4,512,192]{1,2,0:T(8,128)S(1)} %fusion.6), kind=kOutput, calls=%fused_computation.2 | convolution fusion | flops 2416312320 | bytes 8912896 | tf_op jit(solution)/shard_map/lqk,lkr->lqr/dot_general | solution.py:61
  (35 shorter events, 12.0 us)
Async XLA Ops:
  0.0 6.4 %copy-start.8 = (s32[2]{0:T(128)S(1)}, s32[2]{0:T(128)}, u32[]{:S(2)}) copy-start(s32[2]{0:T(128)} %constant.10) | copy-start | bytes 28
  0.0 6.5 %copy-start.9 = (s32[2]{0:T(128)S(1)}, s32[2]{0:T(128)}, u32[]{:S(2)}) copy-start(s32[2]{0:T(128)} %constant.13) | copy-start | bytes 28
  0.0 6.3 %copy-start.7 = (s32[4,512]{1,0:T(4,128)S(1)}, s32[4,512]{1,0:T(4,128)}, u32[]{:S(2)}) copy-start(s32[4,512]{1,0:T(4,128)} %param.6) | copy-start | bytes 24580
  18.9 9.7 %copy-start.5 = (f32[4,192,384]{2,1,0:T(8,128)S(1)}, f32[4,192,384]{2,1,0:T(8,128)}, u32[]{:S(2)}) copy-start(f32[4,192,384]{2,1,0:T(8,128)} %get-tuple-element.10) | copy-start | bytes 3538948
  32.6 3.8 %copy-start.4 = (f32[4,192,384]{2,1,0:T(8,128)S(1)}, f32[4,192,384]{2,1,0:T(8,128)}, u32[]{:S(2)}) copy-start(f32[4,192,384]{2,1,0:T(8,128)} %get-tuple-element.9) | copy-start | bytes 3538948
  40.4 6.9 %copy-start.3 = (f32[4,192,384]{2,1,0:T(8,128)S(1)}, f32[4,192,384]{2,1,0:T(8,128)}, u32[]{:S(2)}) copy-start(f32[4,192,384]{2,1,0:T(8,128)} %get-tuple-element.8) | copy-start | bytes 3538948
  44.3 37.5 %collective-permute-start = (f32[4,192,512]{2,1,0:T(8,128)S(1)}, f32[4,192,512]{2,1,0:T(8,128)S(1)}, u32[]{:S(2)}, u32[]{:S(2)}) collective-permute-start(f32[4,192,512]{2,1,0:T(8,128)S(1)} %bitcast.59), channel_id=1, source_target_pairs={{0,4},{4,0},{8,12},{12,8},{16,20},{20,16},{24,28},{28,24},{1,5},{5... | collective-permute-start | bytes 4718600 | tf_op jit(solution)/shard_map/ppermute | solution.py:12
  48.9 36.3 %copy-start.2 = (f32[4,192,384]{2,1,0:T(8,128)S(1)}, f32[4,192,384]{2,1,0:T(8,128)}, u32[]{:S(2)}) copy-start(f32[4,192,384]{2,1,0:T(8,128)} %get-tuple-element.7) | copy-start | bytes 3538948
  83.4 35.6 %collective-permute-start.1 = (f32[4,192,512]{2,1,0:T(8,128)S(1)}, f32[4,192,512]{2,1,0:T(8,128)S(1)}, u32[]{:S(2)}, u32[]{:S(2)}) collective-permute-start(f32[4,192,512]{2,1,0:T(8,128)S(1)} %bitcast.60), channel_id=1, source_target_pairs={{0,8},{4,12},{8,0},{12,4},{16,24},{20,28},{24,16},{28,20},{1,9},{5... | collective-permute-start | bytes 4718600 | tf_op jit(solution)/shard_map/ppermute | solution.py:12
  86.8 36.6 %copy-start.1 = (f32[4,192,384]{2,1,0:T(8,128)S(1)}, f32[4,192,384]{2,1,0:T(8,128)}, u32[]{:S(2)}) copy-start(f32[4,192,384]{2,1,0:T(8,128)} %get-tuple-element.6) | copy-start | bytes 3538948
  120.8 69.4 %collective-permute-start.2 = (f32[4,192,512]{2,1,0:T(8,128)S(1)}, f32[4,192,512]{2,1,0:T(8,128)S(1)}, u32[]{:S(2)}, u32[]{:S(2)}) collective-permute-start(f32[4,192,512]{2,1,0:T(8,128)S(1)} %bitcast.61), channel_id=1, source_target_pairs={{0,16},{4,20},{8,24},{12,28},{16,0},{20,4},{24,8},{28,12},{1,17},{... | collective-permute-start | bytes 4718600 | tf_op jit(solution)/shard_map/ppermute | solution.py:12
  125.0 66.9 %copy-start = (f32[4,192,384]{2,1,0:T(8,128)S(1)}, f32[4,192,384]{2,1,0:T(8,128)}, u32[]{:S(2)}) copy-start(f32[4,192,384]{2,1,0:T(8,128)} %get-tuple-element.11) | copy-start | bytes 3538948
  191.8 3.5 %collective-permute-start.3 = (f32[4,192,512]{2,1,0:T(8,128)S(1)}, f32[4,192,512]{2,1,0:T(8,128)S(1)}, u32[]{:S(2)}, u32[]{:S(2)}) collective-permute-start(f32[4,192,512]{2,1,0:T(8,128)S(1)} %bitcast.62), channel_id=1, source_target_pairs={{0,1},{1,0},{2,3},{3,2},{4,5},{5,4},{6,7},{7,6},{8,9},{9,8},{10,11... | collective-permute-start | bytes 4718600 | tf_op jit(solution)/shard_map/ppermute | solution.py:12
  193.5 5.7 %copy-start.6 = (f32[4,512,192]{1,2,0:T(8,128)S(1)}, f32[4,512,192]{1,2,0:T(8,128)}, u32[]{:S(2)}) copy-start(f32[4,512,192]{1,2,0:T(8,128)} %param.9) | copy-start | bytes 4718596
  198.1 36.8 %collective-permute-start.4 = (f32[4,192,512]{2,1,0:T(8,128)}, f32[4,192,512]{2,1,0:T(8,128)}, u32[]{:S(2)}, u32[]{:S(2)}) collective-permute-start(f32[4,192,512]{2,1,0:T(8,128)} %bitcast.22), channel_id=1, source_target_pairs={{0,2},{1,3},{2,0},{3,1},{4,6},{5,7},{6,4},{7,5},{8,10},{9,11},{10,... | collective-permute-start | bytes 4718600 | tf_op jit(solution)/shard_map/ppermute | solution.py:12
where the time goes:
time: 243 us
  waiting for transfers between devices  152 us (63%)
  matrix products  48.1 us (20%)
  local copies, waits for them, and re-layouts  33.2 us (14%)
  starting transfers between devices  8.76 us (4%)
    ppermute x5, waiting for transfers between devices, from_partner(): return lax.ppermute(value, axis, pairs)  152 us
    unnamed x26, local copies, waits for them, and re-layouts  24.3 us
    dot_general x7, matrix products, combine(): jnp.einsum('nij,njr->nir', blocks[:, :, skel_size:], other, precision=PRE...  18.6 us
    dot_general x7, matrix products, combine(): jnp.einsum('nij,njr->nir', blocks[:, :, :skel_size], own, precision=PRECISE)  14.8 us
    dot_general x1, matrix products, on_device(): jnp.einsum('lqk,lqr->lkr', placed_in, rhs_grid.reshape(leaf_count, leaf_r...  9.73 us
    ppermute x5, starting transfers between devices, from_partner(): return lax.ppermute(value, axis, pairs)  8.76 us
    squeeze x1, local copies, waits for them, and re-layouts, on_device(): current = combine(transfer[first_col + bit_pos], current, remote)  6.34 us
    dot_general x1, matrix products, on_device(): result = jnp.einsum('lqk,lkr->lqr', placed_out, skeleton, precision=PRECISE)  5.01 us
  transfers between devices with their start and end apart: 5, of which 5 were waited for; matrix products, arithmetic and copies ran while one was open for 9% of the time, Pallas kernels for 0%

commit v1 on v0

v1 whole, which is shorter than its diff:
```python
import functools

import jax
import jax.numpy as jnp
from jax import lax
from jax.experimental import pallas as pl
from jax.experimental.pallas import tpu as pltpu
from jax.sharding import PartitionSpec as P

F32 = jnp.float32
BF16 = jnp.bfloat16
WIDTH = 128


def split(value):
    high = value.astype(BF16)
    return high, (value - high.astype(F32)).astype(BF16)


def dot(a, b):
    return jnp.dot(a, b, preferred_element_type=F32)


def dot3(a_parts, b_parts):
    (a_high, a_low), (b_high, b_low) = a_parts, b_parts
    return dot(a_high, b_high) + (dot(a_high, b_low) + dot(a_low, b_high))


def partner_id(axis, bit_pos):
    mask = 2**bit_pos
    here = lax.axis_index(axis)
    return {axis: here + mask * (1 - 2 * ((here // mask) % 2))}


def kernel(
    stages, offsets, low_bits,
    rhs, order, source, transfer, target, out,
    rhs_v, source_v, target_v, transfer_v, in_high, in_low, out_high, out_low,
    sent, received, staged, rhs_sem, load_sem, transfer_sem, send_sem, recv_sem, out_sem,
):
    leaf_count, leaf_rows = order.shape
    chunks = rhs_v.shape[0]
    units = leaf_count * chunks

    load_source = pltpu.make_async_copy(source, source_v, load_sem.at[0])
    load_target = pltpu.make_async_copy(target, target_v, load_sem.at[1])

    def load_rhs(chunk):
        return pltpu.make_async_copy(
            rhs.at[:, pl.ds(pl.multiple_of(chunk * WIDTH, WIDTH), WIDTH)], rhs_v.at[chunk], rhs_sem.at[chunk]
        )

    def load_transfer(level):
        return pltpu.make_async_copy(transfer.at[level], transfer_v.at[level], transfer_sem.at[level])

    levels = transfer.shape[0]
    load_source.start()
    load_rhs(0).start()
    for level in range(low_bits):
        load_transfer(level).start()
    for level in range(low_bits, levels):
        load_transfer(level).start()
    for chunk in range(1, chunks):
        load_rhs(chunk).start()
    load_target.start()

    barrier = pltpu.get_barrier_semaphore()
    for stage in stages:
        pl.semaphore_signal(barrier, inc=1, device_id=partner_id(*stage), device_id_type=pl.DeviceIdType.MESH)

    def selection(leaf):
        grid_row = lax.broadcasted_iota(jnp.int32, (leaf_rows, leaf_rows), 0)
        named = jnp.broadcast_to(order[pl.ds(leaf, 1), :], (leaf_rows, leaf_rows))
        return jnp.where(grid_row == named, 1.0, 0.0).astype(BF16)

    def place_in(leaf):
        chosen = selection(leaf)
        for part, kept in zip(split(source_v[leaf].T), (in_high, in_low)):
            kept[leaf] = lax.dot_general(
                part, chosen, (((1,), (1,)), ((), ())), preferred_element_type=F32
            ).astype(BF16)

    def place_out(leaf):
        chosen = selection(leaf)
        for part, kept in zip(split(target_v[leaf]), (out_high, out_low)):
            kept[leaf] = dot(chosen, part).astype(BF16)

    def exchange(stage, unit):
        return pltpu.make_async_remote_copy(
            src_ref=sent.at[stage, unit],
            dst_ref=received.at[stage, unit],
            send_sem=send_sem.at[stage, unit],
            recv_sem=recv_sem.at[stage, unit],
            device_id=partner_id(*stages[stage]),
            device_id_type=pl.DeviceIdType.MESH,
        )

    def write_out(unit):
        leaf, chunk = unit % leaf_count, unit // leaf_count
        return pltpu.make_async_copy(
            staged.at[unit],
            out.at[
                pl.ds(pl.multiple_of(leaf * leaf_rows, leaf_rows), leaf_rows),
                pl.ds(pl.multiple_of(chunk * WIDTH, WIDTH), WIDTH),
            ],
            out_sem.at[unit],
        )

    def combine(level, node, own, other):
        return dot3(split(transfer_v[level, node]), split(jnp.concatenate([own, other], axis=0)))

    def enter(chunk):
        load_rhs(chunk).wait()
        current = []
        for leaf in range(leaf_count):
            rows = rhs_v[chunk, pl.ds(leaf * leaf_rows, leaf_rows), :]
            current.append(dot3((in_high[leaf], in_low[leaf]), split(rows)))
        for level in range(low_bits):
            current = [
                combine(level, node, current[node], current[node ^ 2**level]) for node in range(leaf_count)
            ]
        for node in range(leaf_count):
            unit = chunk * leaf_count + node
            sent[0, unit] = current[node]
            exchange(0, unit).start()

    def advance(stage, unit):
        node = unit % leaf_count
        exchange(stage, unit).wait_recv()
        value = combine(low_bits + stage, node, sent[stage, unit], received[stage, unit])
        if stage + 1 < len(stages):
            sent[stage + 1, unit] = value
            exchange(stage + 1, unit).start()
        else:
            staged[unit] = dot3((out_high[node], out_low[node]), split(value))
            write_out(unit).start()

    load_source.wait()
    for leaf in range(leaf_count):
        place_in(leaf)
    for level in range(low_bits):
        load_transfer(level).wait()
    pl.semaphore_wait(barrier, len(stages))
    enter(0)
    for level in range(low_bits, levels):
        load_transfer(level).wait()
    load_target.wait()

    @pl.loop(0, units + offsets[-1])
    def _(tick):
        for stage in range(len(stages)):
            unit = tick - offsets[stage]

            @pl.when((unit >= 0) & (unit < units))
            def _():
                advance(stage, unit)

        @pl.when(tick < leaf_count)
        def _():
            place_out(tick)

        @pl.when((tick % leaf_count == 1) & (tick // leaf_count + 1 < chunks))
        def _():
            enter(tick // leaf_count + 1)

    @pl.loop(0, units)
    def _(unit):
        for stage in range(len(stages)):
            exchange(stage, unit).wait_send()
        write_out(unit).wait()


def on_device(rhs_grid, leaf_order, source_basis, transfer, target_basis):
    leaf_count, leaf_rows = leaf_order.shape
    points, columns = rhs_grid.shape
    rank = source_basis.shape[2]
    levels = transfer.shape[0]
    low_bits = leaf_count.bit_length() - 1
    row_bits = lax.axis_size("row").bit_length() - 1
    col_bits = lax.axis_size("col").bit_length() - 1
    stages = [("row", bit) for bit in range(row_bits)] + [("col", bit) for bit in range(col_bits)]
    count = len(stages)
    offsets = [stage for stage in range(count)]
    offsets[-1] = max(offsets[-1], leaf_count)
    chunks = columns // WIDTH
    units = leaf_count * chunks
    hbm = pl.BlockSpec(memory_space=pl.ANY)
    return pl.pallas_call(
        functools.partial(kernel, stages, offsets, low_bits),
        out_shape=jax.ShapeDtypeStruct((points, columns), F32),
        in_specs=[hbm, pl.BlockSpec(memory_space=pltpu.VMEM), hbm, hbm, hbm],
        out_specs=hbm,
        scratch_shapes=[
            pltpu.VMEM((chunks, points, WIDTH), F32),
            pltpu.VMEM(source_basis.shape, F32),
            pltpu.VMEM(target_basis.shape, F32),
            pltpu.VMEM(transfer.shape, F32),
            pltpu.VMEM((leaf_count, rank, leaf_rows), BF16),
            pltpu.VMEM((leaf_count, rank, leaf_rows), BF16),
            pltpu.VMEM((leaf_count, leaf_rows, rank), BF16),
            pltpu.VMEM((leaf_count, leaf_rows, rank), BF16),
            pltpu.VMEM((count, units, rank, WIDTH), F32),
            pltpu.VMEM((count, units, rank, WIDTH), F32),
            pltpu.VMEM((units, leaf_rows, WIDTH), F32),
            pltpu.SemaphoreType.DMA((chunks,)),
            pltpu.SemaphoreType.DMA((2,)),
            pltpu.SemaphoreType.DMA((levels,)),
            pltpu.SemaphoreType.DMA((count, units)),
            pltpu.SemaphoreType.DMA((count, units)),
            pltpu.SemaphoreType.DMA((units,)),
        ],
        compiler_params=pltpu.CompilerParams(
            collective_id=0, has_side_effects=True, vmem_limit_bytes=60 * 2**20
        ),
    )(rhs_grid, leaf_order, source_basis, transfer, target_basis)


def solution(mesh):
    in_specs = (
        P(("row", "col"), None),
        P(("row", "col"), None),
        P(("row", "col"), None, None),
        P(None, ("row", "col"), None, None),
        P(("row", "col"), None, None),
    )
    out_specs = P(("row", "col"), None)
    return jax.shard_map(
        on_device, mesh=mesh, in_specs=in_specs, out_specs=out_specs, check_vma=False
    )
```

time: 243 us -> 114 us (0.47)
  waiting for transfers between devices: 152 us -> 0 us
  Pallas kernels: 0 us -> 104 us
  matrix products: 48.1 us -> 0 us
  local copies, waits for them, and re-layouts: 33.2 us -> 9.37 us
  starting transfers between devices: 8.76 us -> 0 us
    ppermute x5 -> x0, waiting for transfers between devices: 152 us -> none  [from_partner(): return lax.ppermute(value, axis, pairs)]
    pallas_call x0 -> x1, Pallas kernels: none -> 104 us  [on_device(): pl.pallas_call(functools.partial(kernel, stages, offsets, low_bits), out_...]
    dot_general x16 -> x0, matrix products: 48.1 us -> none  [the longest x7 18.6 us: combine(): jnp.einsum('nij,njr->nir', blocks[:, :, skel_size:], other, precision=PRE...]
    unnamed x26 -> x5, local copies, waits for them, and re-layouts: 24.3 us -> 9.37 us
    ppermute x5 -> x0, starting transfers between devices: 8.76 us -> none  [from_partner(): return lax.ppermute(value, axis, pairs)]
    squeeze x1 -> x0, local copies, waits for them, and re-layouts: 6.34 us -> none  [on_device(): current = combine(transfer[first_col + bit_pos], current, remote)]
    rev x2 -> x0, local copies, waits for them, and re-layouts: 2.54 us -> none  [partner_of(): return halves[:, ::-1].reshape(values.shape)]
  transfers between devices with their start and end apart: 5 -> 0, of which waited for: 5 -> 0; matrix products, arithmetic and copies ran while one was open for 9% -> 0% of each run, Pallas kernels for 0% -> 0%
where the time goes in v1:
time: 114 us; the launch traced here: 113 us
  Pallas kernels  104 us (91%)
  local copies, waits for them, and re-layouts  9.37 us (8%)
    pallas_call x1, Pallas kernels, on_device(): pl.pallas_call(functools.partial(kernel, stages, offsets, low_bits), out_...  104 us
    unnamed x5, local copies, waits for them, and re-layouts  9.37 us

profile of v1, /device:TPU:0, one launch (start us, length us, event | category | flops | bytes accessed | tf_op | source)
XLA Modules:
  0.0 113.3 jit_solution(14664012406686123251)
XLA Ops:
  0.0 0.0 copy-start
  0.0 2.9 %copy.6.source = f32[4,512,192]{2,1,0:T(8,128)} copy(f32[4,512,192]{1,2,0:T(8,128)} %param.7) | data formatting | bytes 3145728 | tf_op args[2]
  2.9 0.0 copy-done
  2.9 1.8 %copy.7.target = f32[4,512,192]{2,1,0:T(8,128)} copy(f32[4,512,192]{1,2,0:T(8,128)S(1)} %copy-done) | data formatting | bytes 3145728 | tf_op args[4]
  4.7 103.9 %shard_map.55 = f32[2048,512]{1,0:T(8,128)} custom-call(f32[2048,512]{1,0:T(8,128)} %rhs.1, s32[4,512]{1,0:T(4,128)} %order.1, f32[4,512,192]{2,1,0:T(8,128)} %copy.6.source, f32[7,4,192,384]{3,2,1,0:T(8,128)} %transfer.1, f32[4,512,192]{2,1,0:T(8,128)} %copy.7.target), custom_call_target="tpu_custom_call" | custom-call | tf_op jit(solution)/shard_map/pallas_call | solution.py:188
  108.7 4.6 %copy.9 = f32[2048,512]{1,0:T(8,128)} copy(f32[2048,512]{1,0:T(8,128)} %shard_map.55) | data formatting | bytes 8388608
Async XLA Ops:
  0.0 2.9 %copy-start = (f32[4,512,192]{1,2,0:T(8,128)S(1)}, f32[4,512,192]{1,2,0:T(8,128)}, u32[]{:S(2)}) copy-start(f32[4,512,192]{1,2,0:T(8,128)} %param.9) | copy-start | bytes 4718596

commit v2 on v1

v2 whole, which is shorter than its diff:
```python
import functools

import jax
import jax.numpy as jnp
from jax import lax
from jax.experimental import pallas as pl
from jax.experimental.pallas import tpu as pltpu
from jax.sharding import PartitionSpec as P

F32 = jnp.float32
BF16 = jnp.bfloat16
WIDTH = 128
MIDDLE = 2
FAR = 3
PLACE_AT = 6


def split(value):
    high = value.astype(BF16)
    return high, (value - high.astype(F32)).astype(BF16)


def dot(a, b):
    return jnp.dot(a, b, preferred_element_type=F32)


def dot3(a_parts, b_parts):
    (a_high, a_low), (b_high, b_low) = a_parts, b_parts
    width = b_high.shape[1]
    both = dot(a_high, jnp.concatenate([b_high, b_low], axis=1))
    return both[:, :width] + (both[:, width:] + dot(a_low, b_high))


def partner_id(axis, bit_pos):
    mask = 2**bit_pos
    here = lax.axis_index(axis)
    return {axis: here + mask * (1 - 2 * ((here // mask) % 2))}


def kernel(
    stages, offsets, low_bits,
    rhs, order, source, transfer, target, out, placed,
    rhs_v, source_v, target_v, transfer_v, in_high, in_low, placed_v,
    sent, received, staged, rhs_sem, load_sem, transfer_sem, send_sem, recv_sem, out_sem, placed_sem,
):
    leaf_count, leaf_rows = order.shape
    chunks = rhs_v.shape[0]
    units = leaf_count * chunks

    load_target = pltpu.make_async_copy(target, target_v, load_sem.at[leaf_count])

    def load_source(leaf):
        return pltpu.make_async_copy(source.at[leaf], source_v.at[leaf], load_sem.at[leaf])

    def load_rhs(chunk):
        return pltpu.make_async_copy(
            rhs.at[:, pl.ds(pl.multiple_of(chunk * WIDTH, WIDTH), WIDTH)], rhs_v.at[chunk], rhs_sem.at[chunk]
        )

    def load_transfer(level):
        return pltpu.make_async_copy(transfer.at[level], transfer_v.at[level], transfer_sem.at[level])

    levels = transfer.shape[0]
    for leaf in range(leaf_count):
        load_source(leaf).start()
    load_rhs(0).start()
    for level in range(low_bits + 2):
        load_transfer(level).start()
    load_rhs(1).start()
    for level in range(low_bits + 2, levels):
        load_transfer(level).start()
    for chunk in range(2, chunks):
        load_rhs(chunk).start()
    load_target.start()

    barrier = pltpu.get_barrier_semaphore()
    for stage in stages:
        pl.semaphore_signal(barrier, inc=1, device_id=partner_id(*stage), device_id_type=pl.DeviceIdType.MESH)

    def selection(leaf):
        grid_row = lax.broadcasted_iota(jnp.int32, (leaf_rows, leaf_rows), 0)
        named = jnp.broadcast_to(order[pl.ds(leaf, 1), :], (leaf_rows, leaf_rows))
        return jnp.where(grid_row == named, 1.0, 0.0).astype(BF16)

    def place_in(leaf):
        parts = jnp.concatenate(split(source_v[leaf]), axis=0)
        rows = lax.dot_general(
            parts, selection(leaf), (((1,), (1,)), ((), ())), preferred_element_type=F32
        ).astype(BF16)
        in_high[leaf] = rows[: source_v.shape[1]]
        in_low[leaf] = rows[source_v.shape[1] :]

    def place_out(leaf):
        chosen = selection(leaf)
        for index, part in enumerate(split(target_v[leaf])):
            placed_v[leaf, index] = lax.dot_general(
                chosen, part, (((1,), (1,)), ((), ())), preferred_element_type=F32
            ).astype(BF16)
        write_placed(leaf).start()

    def write_placed(leaf):
        return pltpu.make_async_copy(placed_v.at[leaf], placed.at[leaf], placed_sem.at[leaf])

    def exchange(stage, unit):
        return pltpu.make_async_remote_copy(
            src_ref=sent.at[stage, unit],
            dst_ref=received.at[stage, unit],
            send_sem=send_sem.at[stage, unit],
            recv_sem=recv_sem.at[stage, unit],
            device_id=partner_id(*stages[stage]),
            device_id_type=pl.DeviceIdType.MESH,
        )

    def write_out(unit):
        leaf, chunk = unit % leaf_count, unit // leaf_count
        return pltpu.make_async_copy(
            staged.at[unit],
            out.at[leaf, :, :, pl.ds(pl.multiple_of(chunk * WIDTH, WIDTH), WIDTH)],
            out_sem.at[unit],
        )

    def combine(level, node, own, other):
        return dot3(split(transfer_v[level, node]), split(jnp.concatenate([own, other], axis=0)))

    def enter(chunk):
        load_rhs(chunk).wait()
        current = []
        for leaf in range(leaf_count):
            rows = rhs_v[chunk, pl.ds(leaf * leaf_rows, leaf_rows), :]
            current.append(dot3((in_high[leaf], in_low[leaf]), split(rows)))
        for level in range(low_bits - 1):
            current = [
                combine(level, node, current[node], current[node ^ 2**level]) for node in range(leaf_count)
            ]
        last = low_bits - 1
        for node in range(leaf_count):
            unit = chunk * leaf_count + node
            if low_bits:
                sent[0, unit] = combine(last, node, current[node], current[node ^ 2**last])
            else:
                sent[0, unit] = current[node]
            exchange(0, unit).start()

    def advance(stage, unit):
        node = unit % leaf_count
        exchange(stage, unit).wait_recv()
        value = combine(low_bits + stage, node, sent[stage, unit], received[stage, unit])
        if stage + 1 < len(stages):
            sent[stage + 1, unit] = value
            exchange(stage + 1, unit).start()
        else:
            for index, part in enumerate(split(value)):
                staged[unit, index] = part
            write_out(unit).start()

    for leaf in range(leaf_count):
        load_source(leaf).wait()
        place_in(leaf)
    for level in range(low_bits):
        load_transfer(level).wait()
    pl.semaphore_wait(barrier, len(stages))
    enter(0)

    near = [stage for stage in range(len(stages)) if stages[stage] == ("col", 0)]
    turns = near + [stage for stage in reversed(range(len(stages))) if stage not in near]

    @pl.loop(0, units + offsets[-1])
    def _(tick):
        for stage in turns:
            unit = tick - offsets[stage]

            @pl.when(unit == 0)
            def _():
                load_transfer(low_bits + stage).wait()

            @pl.when((unit >= 0) & (unit < units))
            def _():
                advance(stage, unit)

        @pl.when(tick == PLACE_AT - 1)
        def _():
            load_target.wait()

        @pl.when((tick >= PLACE_AT) & (tick < PLACE_AT + leaf_count))
        def _():
            place_out(tick - PLACE_AT)

        @pl.when((tick % leaf_count == 1) & (tick // leaf_count + 1 < chunks))
        def _():
            enter(tick // leaf_count + 1)

    @pl.loop(0, units)
    def _(unit):
        for stage in range(len(stages)):
            exchange(stage, unit).wait_send()
        write_out(unit).wait()

    @pl.loop(0, leaf_count)
    def _(leaf):
        write_placed(leaf).wait()


def output_kernel(placed, skeleton, out, placed_v, skeleton_v, out_v, placed_sem, skeleton_sem, out_sem):
    leaf_count, _, leaf_rows, _ = placed_v.shape

    def loads(leaf):
        return (
            pltpu.make_async_copy(placed.at[leaf], placed_v.at[leaf], placed_sem.at[leaf]),
            pltpu.make_async_copy(skeleton.at[leaf], skeleton_v.at[leaf], skeleton_sem.at[leaf]),
        )

    def store(leaf):
        return pltpu.make_async_copy(out_v.at[leaf], out.at[pl.ds(leaf * leaf_rows, leaf_rows), :], out_sem.at[leaf])

    for leaf in range(leaf_count):
        for copy in loads(leaf):
            copy.start()
    for leaf in range(leaf_count):
        for copy in loads(leaf):
            copy.wait()
        out_v[leaf] = dot3((placed_v[leaf, 0], placed_v[leaf, 1]), (skeleton_v[leaf, 0], skeleton_v[leaf, 1]))
        store(leaf).start()
    for leaf in range(leaf_count):
        store(leaf).wait()


def on_device(rhs_grid, leaf_order, source_basis, transfer, target_basis):
    leaf_count, leaf_rows = leaf_order.shape
    points, columns = rhs_grid.shape
    rank = source_basis.shape[2]
    levels = transfer.shape[0]
    low_bits = leaf_count.bit_length() - 1
    row_bits = lax.axis_size("row").bit_length() - 1
    col_bits = lax.axis_size("col").bit_length() - 1
    stages = [("row", bit) for bit in range(row_bits)] + [("col", bit) for bit in range(col_bits)]
    count = len(stages)
    offsets = [0]
    for axis, bit in stages[1:]:
        if axis == "col":
            offsets.append(offsets[-1] + 1)
        else:
            offsets.append(offsets[-1] + (FAR if bit == row_bits - 1 else MIDDLE))
    chunks = columns // WIDTH
    units = leaf_count * chunks
    hbm = pl.BlockSpec(memory_space=pl.ANY)
    skeleton, placed = pl.pallas_call(
        functools.partial(kernel, stages, offsets, low_bits),
        out_shape=[
            jax.ShapeDtypeStruct((leaf_count, 2, rank, columns), BF16),
            jax.ShapeDtypeStruct((leaf_count, 2, leaf_rows, rank), BF16),
        ],
        in_specs=[hbm, pl.BlockSpec(memory_space=pltpu.VMEM), hbm, hbm, hbm],
        out_specs=[hbm, hbm],
        scratch_shapes=[
            pltpu.VMEM((chunks, points, WIDTH), F32),
            pltpu.VMEM((leaf_count, rank, leaf_rows), F32),
            pltpu.VMEM((leaf_count, rank, leaf_rows), F32),
            pltpu.VMEM(transfer.shape, F32),
            pltpu.VMEM((leaf_count, rank, leaf_rows), BF16),
            pltpu.VMEM((leaf_count, rank, leaf_rows), BF16),
            pltpu.VMEM((leaf_count, 2, leaf_rows, rank), BF16),
            pltpu.VMEM((count, units, rank, WIDTH), F32),
            pltpu.VMEM((count, units, rank, WIDTH), F32),
            pltpu.VMEM((units, 2, rank, WIDTH), BF16),
            pltpu.SemaphoreType.DMA((chunks,)),
            pltpu.SemaphoreType.DMA((leaf_count + 1,)),
            pltpu.SemaphoreType.DMA((levels,)),
            pltpu.SemaphoreType.DMA((count, units)),
            pltpu.SemaphoreType.DMA((count, units)),
            pltpu.SemaphoreType.DMA((units,)),
            pltpu.SemaphoreType.DMA((leaf_count,)),
        ],
        compiler_params=pltpu.CompilerParams(
            collective_id=0, has_side_effects=True, vmem_limit_bytes=56 * 2**20
        ),
    )(rhs_grid, leaf_order, source_basis.swapaxes(1, 2), transfer, target_basis.swapaxes(1, 2))
    return pl.pallas_call(
        output_kernel,
        out_shape=jax.ShapeDtypeStruct((points, columns), F32),
        in_specs=[hbm, hbm],
        out_specs=hbm,
        scratch_shapes=[
            pltpu.VMEM(placed.shape, BF16),
            pltpu.VMEM(skeleton.shape, BF16),
            pltpu.VMEM((leaf_count, leaf_rows, columns), F32),
            pltpu.SemaphoreType.DMA((leaf_count,)),
            pltpu.SemaphoreType.DMA((leaf_count,)),
            pltpu.SemaphoreType.DMA((leaf_count,)),
        ],
        compiler_params=pltpu.CompilerParams(vmem_limit_bytes=56 * 2**20),
    )(placed, skeleton)


def solution(mesh):
    in_specs = (
        P(("row", "col"), None),
        P(("row", "col"), None),
        P(("row", "col"), None, None),
        P(None, ("row", "col"), None, None),
        P(("row", "col"), None, None),
    )
    out_specs = P(("row", "col"), None)
    return jax.shard_map(
        on_device, mesh=mesh, in_specs=in_specs, out_specs=out_specs, check_vma=False
    )
```

time: 114 us -> 101 us (0.89)
  local copies, waits for them, and re-layouts: 9.37 us -> 0 us
  Pallas kernels: 104 us -> 101 us
    unnamed x5 -> x0, local copies, waits for them, and re-layouts: 9.37 us -> none
    pallas_call x1, Pallas kernels: 104 us -> 96.3 us  [on_device(): pl.pallas_call(functools.partial(kernel, stages, offsets, low_bits), out_...]
    pallas_call x0 -> x1, Pallas kernels: none -> 4.48 us  [on_device(): pl.pallas_call(output_kernel, out_shape=jax.ShapeDtypeStruct((points, col...]
where the time goes in v2:
time: 101 us
  Pallas kernels  101 us (100%)
    pallas_call x1, Pallas kernels, on_device(): pl.pallas_call(functools.partial(kernel, stages, offsets, low_bits), out_...  96.3 us
    pallas_call x1, Pallas kernels, on_device(): pl.pallas_call(output_kernel, out_shape=jax.ShapeDtypeStruct((points, col...  4.48 us

profile of v2, /device:TPU:0, one launch (start us, length us, event | category | flops | bytes accessed | tf_op | source)
XLA Modules:
  0.0 100.8 jit_solution(2544418153323498631)
XLA Ops:
  0.0 96.3 %shard_map.55 = (bf16[4,2,192,512]{3,2,1,0:T(8,128)(2,1)}, bf16[4,2,512,192]{3,2,1,0:T(8,128)(2,1)}) custom-call(f32[2048,512]{1,0:T(8,128)} %rhs.1, s32[4,512]{1,0:T(4,128)} %order.1, f32[4,192,512]{2,1,0:T(8,128)} %bitcast.2, f32[7,4,192,384]{3,2,1,0:T(8,128)} %transfer.1, f32[4,192,512]{2,1,0:T(8,128)} %bitcast.3), custom_call_target="tpu_custom_call" | custom-call | tf_op jit(solution)/shard_map/pallas_call | solution.py:246
  96.3 4.5 %shard_map.56 = f32[2048,512]{1,0:T(8,128)} custom-call(bf16[4,2,512,192]{3,2,1,0:T(8,128)(2,1)} %get-tuple-element.7.placed, bf16[4,2,192,512]{3,2,1,0:T(8,128)(2,1)} %get-tuple-element.8.skeleton), custom_call_target="tpu_custom_call" | custom-call | tf_op jit(solution)/shard_map/pallas_call | solution.py:277
